TPU v7x, 256 devices: a whole 4x4x8 slice. The times are simulated.
256 devices in a mesh: node: 16 (over x, z_hi), tm: 16 (over z_lo, y, core).
Axes of the slice: x: 4, y: 4, z: 8 (z_hi: 4, z_lo: 2; z = z_hi * 2 + z_lo), core: 2. Of those that a mesh axis runs over, the one named last changes fastest.
Arguments:
- codes: int32 [65536, 2048], P('node', 'tm'), may hold values from -127 to 127
- node_scale: float32 [65536], P('node'), may hold values from 0.002 to 0.02
- basis: bfloat16 [65536, 128], P('node'), may hold values from -0.0234375 to 0.0234375
- regular: float32 [8384], replicated, may hold values from 0.05 to 0.5
- feature_order: int32 [8384], replicated, may hold values from 0 to 8383, each once
- panel_inverse: float32 [2, 262, 262], replicated, may hold values from -0.06 to 1.2
Outputs:
- schur: float32 [8384, 8384], P('node', 'tm')
Inputs may be any that keep to these rules, and one draw needn't show every extreme that they name: `feature_order`: a permutation: every feature stands at exactly one position.
All inputs are finite; a program needn't handle non-finite values.
Results may differ from a plain program's by a relative error of at most 0.0051.
Values sent between devices are 32-bit elements; how exact they have to be, the bound alone decides.
A program may use at most 64 MiB of HBM per device.

v0:
```python
import jax
import jax.numpy as jnp
import numpy as np
from jax import lax
from jax.sharding import PartitionSpec as P


def from_root(block, axis, source):
    block = jnp.where(lax.axis_index(axis) == source, block, jnp.zeros_like(block))
    return lax.psum(block, axis)


def pair_tables(rank_count):
    former_list = []
    latter_list = []
    for leading in range(rank_count + 1):
        for trailing in range(leading, rank_count + 1):
            if leading < rank_count or trailing < rank_count:
                former_list.append(leading)
                latter_list.append(trailing)
    return (np.array(former_list, np.int32), np.array(latter_list, np.int32))


def selectors(chosen, rank_count):
    former, latter = pair_tables(rank_count)
    leading = jnp.take(jnp.asarray(former), chosen)
    trailing = jnp.take(jnp.asarray(latter), chosen)
    lead_index = jnp.minimum(leading, rank_count - 1)
    trail_index = jnp.minimum(trailing, rank_count - 1)
    lead_keep = (leading < rank_count).astype(jnp.float32)
    trail_keep = (trailing < rank_count).astype(jnp.float32)
    return (lead_index, lead_keep, trail_index, trail_keep)


def make_features(window, picks):
    lead_index, lead_keep, trail_index, trail_keep = picks
    lead_vals = (
        jnp.take(window, lead_index, axis=1) * lead_keep[None, :] + (1.0 - lead_keep)[None, :]
    )
    trail_vals = (
        jnp.take(window, trail_index, axis=1) * trail_keep[None, :] + (1.0 - trail_keep)[None, :]
    )
    return (lead_vals * trail_vals).astype(jnp.bfloat16)


def contract(left_feats, right_feats):
    return lax.dot_general(
        left_feats, right_feats, (((0,), (0,)), ((), ())), preferred_element_type=jnp.float32
    )


def highest(left_mat, right_mat):
    return jnp.dot(
        left_mat, right_mat, precision=lax.Precision.HIGHEST, preferred_element_type=jnp.float32
    )


def per_device(codes, node_scale, basis, regular, feature_order, panel_inverse):
    rank_count = basis.shape[1]
    snap_local = codes.shape[1]
    nfeat = regular.shape[0]
    row_size = nfeat // lax.axis_size("node")
    col_size = nfeat // lax.axis_size("tm")
    snap_total = snap_local * lax.axis_size("tm")
    panel_count = panel_inverse.shape[0]
    panel_width = panel_inverse.shape[1]
    scaled_basis = (basis.astype(jnp.float32) * node_scale[:, None]).astype(jnp.bfloat16)
    code_values = codes.astype(jnp.bfloat16)
    row_offset = lax.axis_index("node") * row_size
    col_offset = lax.axis_index("tm") * col_size
    row_picks = selectors(lax.dynamic_slice_in_dim(feature_order, row_offset, row_size), rank_count)
    col_picks = selectors(lax.dynamic_slice_in_dim(feature_order, col_offset, col_size), rank_count)
    empty_tile = jnp.zeros((row_size, col_size), jnp.float32)
    window = code_values
    summed = lax.psum(
        lax.dot_general(
            window, scaled_basis, (((0,), (0,)), ((), ())), preferred_element_type=jnp.float32
        ),
        "node",
    )
    running = empty_tile
    portion = lax.all_gather(summed, "tm", axis=0, tiled=True)
    length = portion.shape[0]
    stride = min(length, 1024)
    for anchor in range(0, length, stride):
        window = portion[anchor : anchor + stride]
        running = running + contract(
            make_features(window, row_picks), make_features(window, col_picks)
        )
    row_global = row_offset + jnp.arange(row_size, dtype=jnp.int32)
    col_global = col_offset + jnp.arange(col_size, dtype=jnp.int32)
    on_diagonal = (row_global[:, None] == col_global[None, :]).astype(jnp.float32)
    row_regular = lax.dynamic_slice_in_dim(regular, row_offset, row_size)
    matrix = running / snap_total + on_diagonal * row_regular[:, None]
    for panel_number in range(panel_count):
        local_panel_lower = panel_number * panel_width
        col_start = local_panel_lower - local_panel_lower // col_size * col_size
        row_start = local_panel_lower - local_panel_lower // row_size * row_size
        col_start, row_start = (col_start, row_start)
        panel_lower = panel_number * panel_width
        left_part = from_root(
            matrix[:, col_start : col_start + panel_width], "tm", panel_lower // col_size
        )
        upper_part = from_root(
            matrix[row_start : row_start + panel_width, :], "node", panel_lower // row_size
        )
        left_part, upper_part = (left_part, upper_part)
        scaled_left = highest(left_part, panel_inverse[panel_number])
        matrix = matrix - highest(scaled_left, upper_part)
    return matrix


def solution(mesh):
    placed = (P("node", "tm"), P("node"), P("node", None), P(), P(), P())
    return jax.shard_map(
        per_device, mesh=mesh, in_specs=placed, out_specs=P("node", "tm"), check_vma=False
    )
```

profile of v0, /device:TPU:8, one launch (start us, length us, event | category | flops | bytes accessed | tf_op | source)
XLA Modules:
  0.0 832.6 jit_solution(677278709692497030)
XLA Ops:
  6.5 3.7 convolution_bitcast_fusion
  10.3 0.9 compare_select_fusion.2
  11.1 155.9 %all-reduce.6.cloned.1.call-done = f32[128,128]{0,1:T(8,128)} async-done(((f32[128,128]{0,1:T(8,128)}), f32[128,128]{0,1:T(8,128)}) %all-reduce.6.cloned.1.call-update) | async-done | bytes 65552 | tf_op jit(solution)/shard_map/psum | solution.py:75
  167.1 3.6 gather_fusion.4
  170.7 3.6 gather_fusion.6
  174.2 3.6 gather_fusion
  177.8 3.6 gather_fusion.2
  182.3 18.9 %all-gather.2.cloned.1.call-done = f32[2048,128]{0,1:T(8,128)} async-done(((f32[128,128]{0,1:T(8,128)}), f32[2048,128]{0,1:T(8,128)}) %all-gather.2.cloned.1.call-update) | async-done | bytes 1048592 | tf_op jit(solution)/shard_map/all_gather | solution.py:82
  201.2 1.3 fusion.55
  202.5 2.5 gather_fusion.7
  205.0 3.3 gather_fusion.3
  208.2 3.3 gather_fusion.9
  211.5 3.3 gather_fusion.11
  214.8 3.3 gather_fusion.1
  218.0 3.3 gather_fusion.8
  221.3 3.3 gather_fusion.5
  224.6 3.3 gather_fusion.10
  227.9 4.9 fusion.18
  233.3 1.9 fusion.17
  235.3 0.9 slice_select_fusion.1
  236.3 0.9 slice_select_fusion.3
  237.5 1.4 fusion.56
  238.8 116.2 %all-reduce.8.cloned.1.call-done = f32[524,262]{1,0:T(8,128)} async-done(((f32[524,262]{1,0:T(8,128)}), f32[524,262]{1,0:T(8,128)}) %all-reduce.8.cloned.1.call-update) | async-done | bytes 549168 | tf_op jit(solution)/shard_map/psum | solution.py:10
  355.0 2.8 fusion.52
  357.9 170.6 %all-reduce.10.cloned.1.call-done = f32[262,524]{1,0:T(8,128)} async-done(((f32[262,524]{1,0:T(8,128)}), f32[262,524]{1,0:T(8,128)}) %all-reduce.10.cloned.1.call-update) | async-done | bytes 549168 | tf_op jit(solution)/shard_map/psum | solution.py:10
  528.4 3.7 convolution_subtract_fusion.1
  532.1 1.2 slice_select_fusion
  533.4 0.9 slice_select_fusion.2
  534.3 113.4 %all-reduce.12.cloned.1.call-done = f32[524,262]{1,0:T(8,128)} async-done(((f32[524,262]{1,0:T(8,128)}), f32[524,262]{1,0:T(8,128)}) %all-reduce.12.cloned.1.call-update) | async-done | bytes 549168 | tf_op jit(solution)/shard_map/psum | solution.py:10
  647.7 2.8 fusion.51
  650.6 170.5 %all-reduce.14.cloned.1.call-done = f32[262,524]{1,0:T(8,128)} async-done(((f32[262,524]{1,0:T(8,128)}), f32[262,524]{1,0:T(8,128)}) %all-reduce.14.cloned.1.call-update) | async-done | bytes 549168 | tf_op jit(solution)/shard_map/psum | solution.py:10
  821.1 4.7 convolution_subtract_fusion
  (41 shorter events, 1.9 us)
Async XLA Ops:
  6.5 160.6 %copy-start.1 = (s32[8384]{0:T(1024)S(1)}, s32[8384]{0:T(1024)}, u32[]{:S(2)}) copy-start(s32[8384]{0:T(1024)} %constant.50.clone2.2) | copy-start | bytes 100612
  6.5 160.5 %all-reduce.6.cloned.1.call-start = ((), (), s32[]{:S(2)}) async-start(), calls=%async_computation | async-start | bytes 131072 | tf_op jit(solution)/shard_map/psum | solution.py:75
  10.2 191.0 %all-gather.2.cloned.1.call-start = ((), (), s32[]{:S(2)}) async-start(), calls=%async_computation.1 | async-start | bytes 1114112 | tf_op jit(solution)/shard_map/all_gather | solution.py:82
  10.3 160.4 %copy-start = (s32[8384]{0:T(1024)S(1)}, s32[8384]{0:T(1024)}, u32[]{:S(2)}) copy-start(s32[8384]{0:T(1024)} %constant.51.clone2.2) | copy-start | bytes 100612
  167.0 188.0 %all-reduce.8.cloned.1.call-start = ((), (), s32[]{:S(2)}) async-start(), calls=%async_computation.2 | async-start | bytes 1622016 | tf_op jit(solution)/shard_map/psum | solution.py:10
  227.9 4.9 copy-start.2
  227.9 4.9 copy-start.3
  227.9 4.9 copy-start.4
  227.9 5.5 copy-start.5
  235.3 2.2 copy-start.7
  236.3 292.2 %all-reduce.10.cloned.1.call-start = ((), (), s32[]{:S(2)}) async-start(), calls=%async_computation.3 | async-start | bytes 1351680 | tf_op jit(solution)/shard_map/psum | solution.py:10
  237.2 410.5 %all-reduce.12.cloned.1.call-start = ((), (), s32[]{:S(2)}) async-start(), calls=%async_computation.4 | async-start | bytes 1622016 | tf_op jit(solution)/shard_map/psum | solution.py:10
  532.1 115.6 %copy-start.6 = (f32[1,262,262]{2,0,1:T(1,128)S(1)}, f32[1,262,262]{2,0,1:T(1,128)}, u32[]{:S(2)}) copy-start(f32[1,262,262]{2,0,1:T(1,128)} %get-tuple-element.27) | copy-start | bytes 823732
  533.3 287.8 %all-reduce.14.cloned.1.call-start = ((), (), s32[]{:S(2)}) async-start(), calls=%async_computation.5 | async-start | bytes 1351680 | tf_op jit(solution)/shard_map/psum | solution.py:10
Sparse Core Ops, SparseCore 0:
  10.3 156.6 all-reduce.5
  168.9 32.2 all-gather.1
  236.4 118.6 all-reduce.7
  357.5 170.8 all-reduce.9
  533.4 114.2 all-reduce.11
  650.2 170.8 all-reduce.13
where the time goes:
time: 833 us
  waiting for transfers between devices  746 us (90%)
  local copies, waits for them, and re-layouts  43.5 us (5%)
  matrix products  24.5 us (3%)
  between operations  13.7 us (2%)
    psum x4, waiting for transfers between devices, from_root(): return lax.psum(block, axis)  571 us
    psum x1, waiting for transfers between devices, per_device(): lax.psum(lax.dot_general(window, scaled_basis, (((0,), (0,)), ((), ())),...  156 us
    all_gather x1, waiting for transfers between devices, per_device(): portion = lax.all_gather(summed, 'tm', axis=0, tiled=True)  18.9 us
  transfers between devices with their start and end apart: 6, of which 6 were waited for; matrix products, arithmetic and copies ran while one was open for 3% of the time, Pallas kernels for 0%

commit v1 on v0

--- a/solution.py
+++ b/solution.py
@@ -7,7 +7,7 @@
 
 def from_root(block, axis, source):
     block = jnp.where(lax.axis_index(axis) == source, block, jnp.zeros_like(block))
-    return lax.psum(block, axis)
+    return jnp.sum(lax.all_gather(block, axis), axis=0)
 
 
 def pair_tables(rank_count):

time: 833 us -> 683 us (0.82); the launches traced: 833 us -> 674 us
  waiting for transfers between devices: 746 us -> 570 us
  other arithmetic: 4.88 us -> 22.7 us
    psum x4 -> x0, waiting for transfers between devices: 571 us -> none  [from_root(): return lax.psum(block, axis)]
    all_gather x0 -> x4, waiting for transfers between devices: none -> 395 us  [from_root(): return jnp.sum(lax.all_gather(block, axis), axis=0)]
    reduce_sum x0 -> x4, other arithmetic: none -> 19.6 us  [from_root(): return jnp.sum(lax.all_gather(block, axis), axis=0)]
  transfers between devices with their start and end apart: 6 -> 6, of which waited for: 6 -> 6; matrix products, arithmetic and copies ran while one was open for 3% -> 5% of each run, Pallas kernels for 0% -> 0%
where the time goes in v1:
time: 683 us; the launch traced here: 674 us
  waiting for transfers between devices  570 us (83%)
  local copies, waits for them, and re-layouts  45.8 us (7%)
  other arithmetic  22.7 us (3%)
  matrix products  21 us (3%)
  between operations  13.8 us (2%)
    all_gather x4, waiting for transfers between devices, from_root(): return jnp.sum(lax.all_gather(block, axis), axis=0)  395 us
    psum x1, waiting for transfers between devices, per_device(): lax.psum(lax.dot_general(window, scaled_basis, (((0,), (0,)), ((), ())),...  156 us
    reduce_sum x4, other arithmetic, from_root(): return jnp.sum(lax.all_gather(block, axis), axis=0)  19.6 us
    all_gather x1, waiting for transfers between devices, per_device(): portion = lax.all_gather(summed, 'tm', axis=0, tiled=True)  18.9 us
  transfers between devices with their start and end apart: 6, of which 6 were waited for; matrix products, arithmetic and copies ran while one was open for 5% of the time, Pallas kernels for 0%

profile of v1, /device:TPU:8, one launch (start us, length us, event | category | flops | bytes accessed | tf_op | source)
XLA Modules:
  0.0 674.3 jit_solution(7983740690641097650)
XLA Ops:
  6.5 3.7 convolution_bitcast_fusion
  11.1 155.9 %all-reduce.2.cloned.1.call-done = f32[128,128]{0,1:T(8,128)} async-done(((f32[128,128]{0,1:T(8,128)}), f32[128,128]{0,1:T(8,128)}) %all-reduce.2.cloned.1.call-update) | async-done | bytes 65552 | tf_op jit(solution)/shard_map/psum | solution.py:75
  167.1 3.6 gather_fusion.4
  170.7 3.6 gather_fusion.6
  174.2 3.6 gather_fusion
  177.8 3.6 gather_fusion.2
  182.3 18.9 %all-gather.14.cloned.1.call-done = f32[2048,128]{0,1:T(8,128)} async-done(((f32[128,128]{0,1:T(8,128)}), f32[2048,128]{0,1:T(8,128)}) %all-gather.14.cloned.1.call-update) | async-done | bytes 1048592 | tf_op jit(solution)/shard_map/all_gather | solution.py:82
  201.2 1.3 fusion.59
  202.5 2.5 gather_fusion.7
  205.0 3.3 gather_fusion.3
  208.2 3.3 gather_fusion.9
  211.5 3.3 gather_fusion.11
  214.8 3.3 gather_fusion.1
  218.0 3.3 gather_fusion.8
  221.3 3.3 gather_fusion.5
  224.6 3.3 gather_fusion.10
  227.9 4.9 fusion.18
  233.3 2.0 fusion.17
  235.4 1.1 copy.17
  237.8 1.4 fusion.60
  239.1 63.4 %all-gather.16.cloned.1.call-done = f32[16,524,262]{1,2,0:T(8,128)} async-done(((f32[1,524,262]{1,2,0:T(8,128)}), f32[16,524,262]{1,2,0:T(8,128)}) %all-gather.16.cloned.1.call-update) | async-done | bytes 8786448 | tf_op jit(solution)/shard_map/all_gather | solution.py:10
  302.6 4.7 reduce_sum.36
  307.3 1.5 fusion.56
  308.8 130.3 %all-gather.18.cloned.1.call-done = f32[16,262,524]{2,1,0:T(8,128)} async-done(((f32[1,262,524]{2,1,0:T(8,128)}), f32[16,262,524]{2,1,0:T(8,128)}) %all-gather.18.cloned.1.call-update) | async-done | bytes 8786448 | tf_op jit(solution)/shard_map/all_gather | solution.py:10
  439.0 5.5 reduce_sum.37
  444.6 3.7 convolution_subtract_fusion.1
  451.0 71.5 %all-gather.20.cloned.1.call-done = f32[16,524,262]{1,2,0:T(8,128)} async-done(((f32[1,524,262]{1,2,0:T(8,128)}), f32[16,524,262]{1,2,0:T(8,128)}) %all-gather.20.cloned.1.call-update) | async-done | bytes 8786448 | tf_op jit(solution)/shard_map/all_gather | solution.py:10
  522.5 4.7 reduce_sum.38
  527.3 1.5 fusion.55
  528.8 130.3 %all-gather.22.cloned.1.call-done = f32[16,262,524]{2,1,0:T(8,128)} async-done(((f32[1,262,524]{2,1,0:T(8,128)}), f32[16,262,524]{2,1,0:T(8,128)}) %all-gather.22.cloned.1.call-update) | async-done | bytes 8786448 | tf_op jit(solution)/shard_map/all_gather | solution.py:10
  659.0 4.7 reduce_sum.39
  663.7 3.7 convolution_subtract_fusion
  (47 shorter events, 6.3 us)
Async XLA Ops:
  6.5 160.6 %copy-start.1 = (s32[8384]{0:T(1024)S(1)}, s32[8384]{0:T(1024)}, u32[]{:S(2)}) copy-start(s32[8384]{0:T(1024)} %constant.27.clone2.2) | copy-start | bytes 100612
  6.5 160.5 %all-reduce.2.cloned.1.call-start = ((), (), s32[]{:S(2)}) async-start(), calls=%async_computation | async-start | bytes 131072 | tf_op jit(solution)/shard_map/psum | solution.py:75
  10.2 191.0 %all-gather.14.cloned.1.call-start = ((), (), s32[]{:S(2)}) async-start(), calls=%async_computation.1 | async-start | bytes 1114112 | tf_op jit(solution)/shard_map/all_gather | solution.py:82
  10.3 160.4 %copy-start = (s32[8384]{0:T(1024)S(1)}, s32[8384]{0:T(1024)}, u32[]{:S(2)}) copy-start(s32[8384]{0:T(1024)} %constant.52.clone2.2) | copy-start | bytes 100612
  167.0 135.5 %all-gather.16.cloned.1.call-start = ((), (), s32[]{:S(2)}) async-start(), calls=%async_computation.2 | async-start | bytes 11489280 | tf_op jit(solution)/shard_map/all_gather | solution.py:10
  227.9 4.9 copy-start.2
  227.9 4.9 copy-start.3
  227.9 4.9 copy-start.4
  227.9 5.5 copy-start.5
  235.4 2.4 copy-start.7
  236.5 202.5 %all-gather.18.cloned.1.call-start = ((), (), s32[]{:S(2)}) async-start(), calls=%async_computation.3 | async-start | bytes 11489280 | tf_op jit(solution)/shard_map/all_gather | solution.py:10
  237.7 284.8 %all-gather.20.cloned.1.call-start = ((), (), s32[]{:S(2)}) async-start(), calls=%async_computation.4 | async-start | bytes 11489280 | tf_op jit(solution)/shard_map/all_gather | solution.py:10
  449.8 209.2 %all-gather.22.cloned.1.call-start = ((), (), s32[]{:S(2)}) async-start(), calls=%async_computation.5 | async-start | bytes 11489280 | tf_op jit(solution)/shard_map/all_gather | solution.py:10
  451.0 76.3 %copy-start.6 = (f32[1,262,262]{2,0,1:T(1,128)S(1)}, f32[1,262,262]{2,0,1:T(1,128)}, u32[]{:S(2)}) copy-start(f32[1,262,262]{2,0,1:T(1,128)} %get-tuple-element.27) | copy-start | bytes 823732
Sparse Core Ops, SparseCore 0:
  10.3 156.6 all-reduce.1
  168.9 32.2 all-gather.13
  236.7 65.8 all-gather.15
  305.2 133.7 all-gather.17
  449.9 72.6 all-gather.19
  525.2 133.7 all-gather.21
